TPU v7x, 32 devices: a whole 2x2x4 slice. The times are simulated.
32 devices in a mesh: dom: 2 (over y), frame: 4 (over z), query: 2 (over x), split: 2 (over core).
Axes of the slice: x: 2, y: 2, z: 4, core: 2. Of those that a mesh axis runs over, the one named last changes fastest.
Arguments:
- frames: bfloat16 [16, 1024, 256], P(('dom', 'frame')), parts along dimension 0, may hold values from -64 to 64
- query_frame: int32 [2048], P(('dom', 'query')), parts along dimension 0, may hold values from 0 to 7, as said below
- query_pixel: int32 [2, 2048], P(None, ('dom', 'query')), parts along dimension 1, may hold values from 0 to 31
- in_weight: bfloat16 [512, 512], replicated, may hold values from -0.25 to 0.25
- conv_weight: float32 [1, 3, 512], replicated, may hold values from -3 to 3
- up_weight: bfloat16 [1, 512, 2048], P(None, None, 'split'), may hold values from -0.25 to 0.25
- down_weight: bfloat16 [1, 2048, 512], P(None, 'split'), may hold values from -0.125 to 0.125
Outputs:
- tokens: bfloat16 [2048, 8, 512], P(('dom', 'query'), 'frame'), parts along dimension 0
There are 2 independent parts, one for each index of `dom`. A program takes and returns all parts, laid end to end along the dimension named above; an argument that names none is the same for every part. Nothing has to cross between parts.
Inputs may be any that keep to these rules, and one draw needn't show every extreme that they name: `query_frame`: within each aligned group of 512 query points (one index of query), at most 384 start frames lie among any aligned 2 frames (one index of frame), and in every group some such frames hold exactly 384.
All inputs are finite; a program needn't handle non-finite values.
Results may differ from a plain program's by a relative error of at most 0.006.
Values may be sent and summed in bfloat16 or wider, within the bound.
No kernel may reach another device: no remote copies, remote signals or barrier semaphores. Data moves between devices by JAX's collectives and lax.ppermute only.
A program may use at most 64 MiB of HBM per device.

v0:
```python
import math
import jax
import jax.numpy as jnp
from jax import lax
from jax.sharding import PartitionSpec as P

SIDE = 32


def with_halo(cells, sides, width):
    for axis, dim in sides:
        count = lax.axis_size(axis)
        ends = count - 1
        head = lax.slice_in_dim(cells, 0, width, axis=dim)
        tail = lax.slice_in_dim(cells, cells.shape[dim] - width, cells.shape[dim], axis=dim)
        cells = jnp.concatenate(
            [
                lax.ppermute(tail, axis, [(i, (i + 1) % count) for i in range(ends)]),
                cells,
                lax.ppermute(head, axis, [((i + 1) % count, i) for i in range(ends)]),
            ],
            axis=dim,
        )
    return cells


def rms_scale(values, epsilon):
    return values / jnp.sqrt(jnp.mean(values * values, axis=-1, keepdims=True) + epsilon)


def on_device(frames, query_frame, query_pixel, in_weight, conv_weight, up_weight, down_weight):
    frame_count, pixel_count, channels = frames.shape
    query_count = query_frame.shape[0]
    width = in_weight.shape[1]
    first_frame = lax.axis_index("frame") * frame_count
    flat_frames = frames.reshape(frame_count * pixel_count, channels)
    pixel_index = query_pixel[0] * SIDE + query_pixel[1]
    local_frame = query_frame - first_frame
    is_owned = (local_frame >= 0) & (local_frame < frame_count)
    column = jnp.where(is_owned, local_frame * pixel_count + pixel_index, -1)
    picker = (
        column[:, None] == jnp.arange(frame_count * pixel_count, dtype=jnp.int32)[None, :]
    ).astype(jnp.bfloat16)
    own_features = jnp.dot(picker, flat_frames, preferred_element_type=jnp.float32)
    devices = lax.axis_size("frame")
    capacity = max(2, 3 * query_count // devices)
    owner = query_frame // frame_count
    order = jnp.arange(query_count, dtype=jnp.int32)
    earlier = (owner[:, None] == owner[None, :]) & (order[None, :] < order[:, None])
    ranking = jnp.sum(earlier.astype(jnp.int32), axis=1)
    slot_pick = (
        (ranking[None, :] == jnp.arange(capacity, dtype=jnp.int32)[:, None]) & is_owned[None, :]
    ).astype(jnp.bfloat16)
    packed = jnp.dot(
        slot_pick, own_features.astype(jnp.bfloat16), preferred_element_type=jnp.float32
    ).astype(jnp.bfloat16)
    every_slot = lax.all_gather(packed, "frame", axis=0, tiled=True)
    source = owner * capacity + ranking
    unpick = (source[:, None] == jnp.arange(devices * capacity, dtype=jnp.int32)[None, :]).astype(
        jnp.bfloat16
    )
    query_features = jnp.dot(unpick, every_slot, preferred_element_type=jnp.float32).astype(
        jnp.bfloat16
    )
    scores = jnp.einsum(
        "qc,tpc->qtp", query_features, frames, preferred_element_type=jnp.float32
    ) * (1.0 / math.sqrt(channels))
    peak = jnp.max(scores, axis=-1, keepdims=True)
    expd = jnp.exp(scores - peak)
    weights = (expd / jnp.sum(expd, axis=-1, keepdims=True)).astype(jnp.bfloat16)
    pooled = jnp.einsum("qtp,tpc->qtc", weights, frames, preferred_element_type=jnp.float32)
    normed = rms_scale(pooled, 1e-06).astype(jnp.bfloat16)
    joined = jnp.concatenate(
        [normed, jnp.broadcast_to(query_features[:, None, :], normed.shape)], axis=-1
    )
    stream = jnp.einsum("qtc,cd->qtd", joined, in_weight, preferred_element_type=jnp.float32)
    rows_total = query_count * frame_count
    level = rms_scale(stream, 1e-05).astype(jnp.bfloat16)
    padded = with_halo(level, (("frame", 1),), 1).astype(jnp.float32)
    taps = conv_weight[0]
    mixed_time = taps[0] * padded[:, :-2] + taps[1] * padded[:, 1:-1] + taps[2] * padded[:, 2:]
    stream = stream + mixed_time
    gated = rms_scale(stream, 1e-05).astype(jnp.bfloat16).reshape(rows_total, width)
    hidden = jax.nn.gelu(jnp.dot(gated, up_weight[0], preferred_element_type=jnp.float32)).astype(
        jnp.bfloat16
    )
    partial_delta = jnp.dot(hidden, down_weight[0], preferred_element_type=jnp.float32)
    summed = lax.psum(partial_delta.astype(jnp.bfloat16), "split").astype(jnp.float32)
    stream = stream + summed.reshape(query_count, frame_count, width)
    return stream.astype(jnp.bfloat16)


def solution(mesh):
    return jax.shard_map(
        on_device,
        mesh=mesh,
        in_specs=(
            P(("dom", "frame"), None, None),
            P(("dom", "query")),
            P(None, ("dom", "query")),
            P(),
            P(),
            P(None, None, "split"),
            P(None, "split", None),
        ),
        out_specs=P(("dom", "query"), "frame", None),
        check_vma=False,
    )
```

profile of v0, /device:TPU:0, one launch (start us, length us, event | category | flops | bytes accessed | tf_op | source)
XLA Modules:
  0.0 102.2 jit_solution(10552802000820765589)
XLA Ops:
  6.5 0.0 copy-start
  6.5 0.0 all-reduce.2.cloned.1.call-start
  6.5 0.8 slice_add_fusion
  7.3 0.7 compare_and_fusion
  8.0 0.7 add_select_fusion
  8.7 0.3 convert_reduce_fusion
  9.0 0.0 copy-done
  9.0 1.2 %convolution_convert_fusion.1 = bf16[384,256]{1,0:T(8,128)(2,1)S(1)} fusion(bf16[2048,256]{1,0:T(8,128)(2,1)S(1)} %bitcast.38, s32[512]{0:T(512)S(1)} %get-tuple-element.13, s32[512]{0:T(512)S(1)} %convert_reduce_fusion, pred[512]{0:T(512)(128)(4,1)S(1)} %compare_and_fusion), kind=kOutput, calls=%fused_computation.38 | convolution fusion | flops 639205376 | bytes 1249792 | tf_op jit(solution)/shard_map/dot_general | solution.py:54
  10.2 21.3 %all_gather.3 = bf16[1536,256]{1,0:T(8,128)(2,1)S(1)} all-gather(bf16[384,256]{1,0:T(8,128)(2,1)S(1)} %convolution_convert_fusion.1), channel_id=1, replica_groups=mesh['dom'=2,'frame'=4,'query'=2,'split'=2] {'frame'}, dimensions={0}, use_global_device_ids=true | all-gather | bytes 983040 | tf_op jit(solution)/shard_map/all_gather | solution.py:57
  31.5 0.7 fusion.23
  32.2 0.1 copy.19
  32.3 3.3 %fusion.57 = (f32[512,2]{0,1:T(2,128)S(1)}, f32[512,2,1024]{2,0,1:T(8,128)}) fusion(bf16[2,1024,256]{2,1,0:T(8,128)(2,1)S(1)} %copy-done, bf16[512,256]{1,0:T(8,128)(2,1)S(1)} %fusion.23), kind=kOutput, calls=%fused_computation.81 | convolution fusion | flops 540017664 | bytes 5509120 | tf_op jit(solution)/shard_map/sub | solution.py:69
  35.6 3.1 %multiply_reduce_fusion.3 = (f32[512,2]{0,1:T(2,128)S(1)}, f32[512,2,256]{0,2,1:T(8,128)S(1)}) fusion(bf16[2,1024,256]{2,1,0:T(8,128)(2,1)S(1)} %copy-done, f32[512,2,1024]{2,0,1:T(8,128)} %get-tuple-element.15, f32[512,2]{0,1:T(2,128)S(1)} %get-tuple-element.14), kind=kOutput, calls=%fused_computation.46 | convolution fusion | flops 539491328 | bytes 6299648 | tf_op jit(solution)/shard_map/qtp,tpc->qtc/dot_general | solution.py:71
  38.7 0.0 copy-start.2
  38.7 0.1 divide_convert_fusion.6
  38.9 0.8 copy-done.2
  39.7 0.8 multiply_reduce_fusion.2
  40.6 0.0 copy-start.1
  40.6 0.2 divide_convert_fusion.2
  40.8 0.1 fusion.55
  40.9 1.6 %collective-permute-start = (bf16[512,1,512]{2,0,1:T(8,128)(2,1)S(1)}, bf16[512,1,512]{2,0,1:T(8,128)(2,1)S(1)}, u32[]{:S(2)}, u32[]{:S(2)}) collective-permute-start(bf16[512,1,512]{2,0,1:T(8,128)(2,1)S(1)} %get-tuple-element.7), channel_id=1, source_target_pairs={{0,4},{4,8},{8,12},{1,5},{5,9},{9,13},{2,6},{6,10},{10,14},{3,7},{... | collective-permute-start | bytes 1572872 | tf_op jit(solution)/shard_map/ppermute | solution.py:18
  42.4 1.5 %collective-permute-start.1 = (bf16[512,1,512]{2,0,1:T(8,128)(2,1)S(1)}, bf16[512,1,512]{2,0,1:T(8,128)(2,1)S(1)}, u32[]{:S(2)}, u32[]{:S(2)}) collective-permute-start(bf16[512,1,512]{2,0,1:T(8,128)(2,1)S(1)} %get-tuple-element.8), channel_id=1, source_target_pairs={{4,0},{8,4},{12,8},{5,1},{9,5},{13,9},{6,2},{10,6},{14,10},{7,3},{... | collective-permute-start | bytes 1572872 | tf_op jit(solution)/shard_map/ppermute | solution.py:20
  43.9 0.0 copy-done.1
  43.9 8.1 %collective-permute-done = bf16[512,1,512]{2,0,1:T(8,128)(2,1)S(1)} collective-permute-done((bf16[512,1,512]{2,0,1:T(8,128)(2,1)S(1)}, bf16[512,1,512]{2,0,1:T(8,128)(2,1)S(1)}, u32[]{:S(2)}, u32[]{:S(2)}) %collective-permute-start) | collective-permute-done | bytes 524320 | tf_op jit(solution)/shard_map/ppermute | solution.py:18
  52.0 4.1 %collective-permute-done.1 = bf16[512,1,512]{2,0,1:T(8,128)(2,1)S(1)} collective-permute-done((bf16[512,1,512]{2,0,1:T(8,128)(2,1)S(1)}, bf16[512,1,512]{2,0,1:T(8,128)(2,1)S(1)}, u32[]{:S(2)}, u32[]{:S(2)}) %collective-permute-start.1) | collective-permute-done | bytes 524320 | tf_op jit(solution)/shard_map/ppermute | solution.py:20
  56.2 0.3 maximum_convert_fusion
  56.5 0.7 multiply_reduce_fusion.1
  57.2 0.2 divide_convert_fusion.1
  57.4 2.0 %copy.21 = bf16[512,2,512]{2,1,0:T(2,128)(2,1)} copy(bf16[512,2,512]{2,0,1:T(8,128)(2,1)S(1)} %divide_convert_fusion.1) | data formatting | bytes 2097152 | tf_op jit(solution)/shard_map/convert_element_type | solution.py:83
  59.5 2.3 %reshape.55 = bf16[1024,512]{1,0:T(8,128)(2,1)} reshape(bf16[512,2,512]{2,1,0:T(2,128)(2,1)} %copy.21) | data formatting | bytes 2097152 | tf_op jit(solution)/shard_map/reshape | solution.py:83
  61.7 5.2 %convolution_convert_fusion = bf16[1024,512]{1,0:T(8,128)(2,1)} fusion(bf16[1024,512]{1,0:T(8,128)(2,1)} %reshape.55, bf16[1,1024,512]{2,1,0:T(8,128)(2,1)} %param.13, bf16[1,512,1024]{2,1,0:T(8,128)(2,1)} %param.12), kind=kOutput, calls=%fused_computation.34 | convolution fusion | flops 2157445120 | bytes 4194304 | tf_op jit(solution)/shard_map/dot_general | solution.py:87
  67.0 2.3 %reshape.56 = bf16[512,2,512]{2,1,0:T(2,128)(2,1)} reshape(bf16[1024,512]{1,0:T(8,128)(2,1)} %convolution_convert_fusion) | data formatting | bytes 2097152 | tf_op jit(solution)/shard_map/reshape | solution.py:89
  69.2 2.4 %copy.22 = bf16[512,2,512]{2,0,1:T(8,128)(2,1)} copy(bf16[512,2,512]{2,1,0:T(2,128)(2,1)} %reshape.56) | data formatting | bytes 2097152 | tf_op jit(solution)/shard_map/reshape | solution.py:89
  71.6 0.0 all-reduce.2.cloned.1.call-update
  71.6 20.1 %all-reduce.2.cloned.1.call-done = bf16[512,2,512]{2,0,1:T(8,128)(2,1)} async-done(((bf16[512,2,512]{2,0,1:T(8,128)(2,1)}), bf16[512,2,512]{2,0,1:T(8,128)(2,1)}) %all-reduce.2.cloned.1.call-update) | async-done | bytes 1048592 | tf_op jit(solution)/shard_map/psum | solution.py:88
  91.7 1.6 %add_convert_fusion = bf16[512,2,512]{2,0,1:T(8,128)(2,1)S(1)} fusion(f32[512,2,512]{2,0,1:T(8,128)S(1)} %get-tuple-element.6, bf16[512,2,512]{2,0,1:T(8,128)(2,1)} %all-reduce.2.cloned.1.call-done), kind=kLoop, calls=%fused_computation.25 | loop fusion | flops 1572864 | bytes 4194304 | tf_op jit(solution)/shard_map/convert_element_type | solution.py:90
  93.3 2.0 %copy.23 = bf16[512,2,512]{2,1,0:T(2,128)(2,1)} copy(bf16[512,2,512]{2,0,1:T(8,128)(2,1)S(1)} %add_convert_fusion) | data formatting | bytes 2097152 | tf_op jit(solution)/shard_map/convert_element_type | solution.py:90
  (6 shorter events, 0.1 us)
Async XLA Ops:
  6.5 2.4 %copy-start = (bf16[2,1024,256]{2,1,0:T(8,128)(2,1)S(1)}, bf16[2,1024,256]{2,1,0:T(8,128)(2,1)}, u32[]{:S(2)}) copy-start(bf16[2,1024,256]{2,1,0:T(8,128)(2,1)} %param.7) | copy-start | bytes 3145732
  6.5 85.2 %all-reduce.2.cloned.1.call-start = ((), (), s32[]{:S(2)}) async-start(), calls=%async_computation | async-start | bytes 2097152 | tf_op jit(solution)/shard_map/psum | solution.py:88
  38.7 1.0 %copy-start.2 = (bf16[512,512]{1,0:T(8,128)(2,1)S(1)}, bf16[512,512]{1,0:T(8,128)(2,1)}, u32[]{:S(2)}) copy-start(bf16[512,512]{1,0:T(8,128)(2,1)} %param.10) | copy-start | bytes 1572868
  40.6 3.4 %copy-start.1 = (f32[1,3,512]{2,0,1:T(1,128)S(1)}, f32[1,3,512]{2,0,1:T(1,128)}, u32[]{:S(2)}) copy-start(f32[1,3,512]{2,0,1:T(1,128)} %param.11) | copy-start | bytes 18436
  40.9 11.2 %collective-permute-start = (bf16[512,1,512]{2,0,1:T(8,128)(2,1)S(1)}, bf16[512,1,512]{2,0,1:T(8,128)(2,1)S(1)}, u32[]{:S(2)}, u32[]{:S(2)}) collective-permute-start(bf16[512,1,512]{2,0,1:T(8,128)(2,1)S(1)} %get-tuple-element.7), channel_id=1, source_target_pairs={{0,4},{4,8},{8,12},{1,5},{5,9},{9,13},{2,6},{6,10},{10,14},{3,7},{... | collective-permute-start | bytes 1572872 | tf_op jit(solution)/shard_map/ppermute | solution.py:18
  42.4 13.7 %collective-permute-start.1 = (bf16[512,1,512]{2,0,1:T(8,128)(2,1)S(1)}, bf16[512,1,512]{2,0,1:T(8,128)(2,1)S(1)}, u32[]{:S(2)}, u32[]{:S(2)}) collective-permute-start(bf16[512,1,512]{2,0,1:T(8,128)(2,1)S(1)} %get-tuple-element.8), channel_id=1, source_target_pairs={{4,0},{8,4},{12,8},{5,1},{9,5},{13,9},{6,2},{10,6},{14,10},{7,3},{... | collective-permute-start | bytes 1572872 | tf_op jit(solution)/shard_map/ppermute | solution.py:20
Sparse Core Ops, SparseCore 0:
  71.7 19.9 all-reduce.1
where the time goes:
time: 103 us; the launch traced here: 102 us
  waiting for transfers between devices  32.4 us (31%)
  blocking collectives  21.3 us (21%)
  matrix products  14.3 us (14%)
  between operations  13.5 us (13%)
  local copies, waits for them, and re-layouts  12.1 us (12%)
  other arithmetic  5.59 us (5%)
  starting transfers between devices  3.05 us (3%)
    all_gather x1, blocking collectives, on_device(): every_slot = lax.all_gather(packed, 'frame', axis=0, tiled=True)  21.3 us
    psum x1, waiting for transfers between devices, on_device(): lax.psum(partial_delta.astype(jnp.bfloat16), 'split').astype(jnp.float32)  20.1 us
    ppermute x1, waiting for transfers between devices, with_halo(): lax.ppermute(tail, axis, [(i, (i + 1) % count) for i in range(ends)])  8.08 us
    dot_general x1, matrix products, on_device(): jnp.dot(hidden, down_weight[0], preferred_element_type=jnp.float32)  5.25 us
    reshape x2, local copies, waits for them, and re-layouts, on_device(): stream = stream + summed.reshape(query_count, frame_count, width)  4.62 us
    ppermute x1, waiting for transfers between devices, with_halo(): lax.ppermute(head, axis, [((i + 1) % count, i) for i in range(ends)])  4.15 us
    sub x1, matrix products, on_device(): expd = jnp.exp(scores - peak)  3.28 us
    dot_general x1, matrix products, on_device(): jnp.einsum('qtp,tpc->qtc', weights, frames, preferred_element_type=jnp.fl...  3.07 us
  transfers between devices with their start and end apart: 3, of which 3 were waited for; matrix products, arithmetic and copies ran while one was open for 0% of the time, Pallas kernels for 0%

commit v1 on v0

--- a/solution.py
+++ b/solution.py
@@ -5,6 +5,27 @@
 from jax.sharding import PartitionSpec as P
 
 SIDE = 32
+
+
+def cycles_draft(point, row_dim):
+    point = jnp.moveaxis(point, 0, row_dim)
+    x_now = point.shape
+    return point.reshape(
+        *x_now[:row_dim], x_now[row_dim] * x_now[row_dim + 1], *x_now[row_dim + 2 :]
+    )
+
+
+def _search_slices(chunk, a_name):
+    full_n = lax.axis_size(a_name)
+    big = chunk[None]
+    for it in range(full_n.bit_length() - 1):
+        low = 1 << it
+        tall = lax.ppermute(big, a_name, [(at, at ^ low) for at in range(full_n)])
+        u1 = jnp.stack([big, tall], axis=0)
+        w1 = lax.axis_index(a_name)
+        shaped = w1 >> it & 1
+        big = jnp.where(shaped == 0, u1, u1[::-1]).reshape(-1, *chunk.shape)
+    return big
 
 
 def with_halo(cells, sides, width):
@@ -54,7 +75,8 @@
     packed = jnp.dot(
         slot_pick, own_features.astype(jnp.bfloat16), preferred_element_type=jnp.float32
     ).astype(jnp.bfloat16)
-    every_slot = lax.all_gather(packed, "frame", axis=0, tiled=True)
+    odd = _search_slices(packed, "frame")
+    every_slot = cycles_draft(odd, 0)
     source = owner * capacity + ranking
     unpick = (source[:, None] == jnp.arange(devices * capacity, dtype=jnp.int32)[None, :]).astype(
         jnp.bfloat16

time: 103 us -> 112 us (1.087)
  waiting for transfers between devices: 32.4 us -> 56.3 us
  blocking collectives: 21.3 us -> 0 us
  starting transfers between devices: 3.05 us -> 9.91 us
    ppermute x0 -> x2, waiting for transfers between devices: none -> 21.7 us  [_search_slices(): tall = lax.ppermute(big, a_name, [(at, at ^ low) for at in range(full_n)])]
    all_gather x1 -> x0, blocking collectives: 21.3 us -> none  [on_device(): every_slot = lax.all_gather(packed, 'frame', axis=0, tiled=True)]
    ppermute x0 -> x2, starting transfers between devices: none -> 5.94 us  [_search_slices(): tall = lax.ppermute(big, a_name, [(at, at ^ low) for at in range(full_n)])]
    ppermute x1, waiting for transfers between devices: 8.08 us -> 9.81 us  [with_halo(): lax.ppermute(tail, axis, [(i, (i + 1) % count) for i in range(ends)])]
  transfers between devices with their start and end apart: 3 -> 5, of which waited for: 3 -> 5; matrix products, arithmetic and copies ran while one was open for 0% -> 0% of each run, Pallas kernels for 0% -> 0%
where the time goes in v1:
time: 112 us
  waiting for transfers between devices  56.3 us (50%)
  matrix products  14.3 us (13%)
  between operations  13.6 us (12%)
  local copies, waits for them, and re-layouts  12.1 us (11%)
  starting transfers between devices  9.91 us (9%)
  other arithmetic  5.94 us (5%)
    ppermute x2, waiting for transfers between devices, _search_slices(): tall = lax.ppermute(big, a_name, [(at, at ^ low) for at in range(full_n)])  21.7 us
    psum x1, waiting for transfers between devices, on_device(): lax.psum(partial_delta.astype(jnp.bfloat16), 'split').astype(jnp.float32)  20.6 us
    ppermute x1, waiting for transfers between devices, with_halo(): lax.ppermute(tail, axis, [(i, (i + 1) % count) for i in range(ends)])  9.81 us
    ppermute x2, starting transfers between devices, _search_slices(): tall = lax.ppermute(big, a_name, [(at, at ^ low) for at in range(full_n)])  5.94 us
    dot_general x1, matrix products, on_device(): jnp.dot(hidden, down_weight[0], preferred_element_type=jnp.float32)  5.25 us
    reshape x2, local copies, waits for them, and re-layouts, on_device(): stream = stream + summed.reshape(query_count, frame_count, width)  4.62 us
    ppermute x1, waiting for transfers between devices, with_halo(): lax.ppermute(head, axis, [((i + 1) % count, i) for i in range(ends)])  4.15 us
    sub x1, matrix products, on_device(): expd = jnp.exp(scores - peak)  3.28 us
  transfers between devices with their start and end apart: 5, of which 5 were waited for; matrix products, arithmetic and copies ran while one was open for 0% of the time, Pallas kernels for 0%

profile of v1, /device:TPU:0, one launch (start us, length us, event | category | flops | bytes accessed | tf_op | source)
XLA Modules:
  0.0 112.1 jit_solution(4409674771107431858)
XLA Ops:
  6.5 0.0 copy-start
  6.5 0.0 all-reduce.2.cloned.1.call-start
  6.5 0.8 slice_add_fusion
  7.3 0.7 compare_and_fusion
  8.0 0.7 add_select_fusion
  8.7 0.3 convert_reduce_fusion
  9.0 0.0 copy-done
  9.0 1.2 %convolution_convert_fusion.1 = bf16[384,256]{1,0:T(8,128)(2,1)S(1)} fusion(bf16[2048,256]{1,0:T(8,128)(2,1)S(1)} %bitcast.47, s32[512]{0:T(512)S(1)} %get-tuple-element.15, s32[512]{0:T(512)S(1)} %convert_reduce_fusion, pred[512]{0:T(512)(128)(4,1)S(1)} %compare_and_fusion), kind=kOutput, calls=%fused_computation.39 | convolution fusion | flops 639205376 | bytes 1249792 | tf_op jit(solution)/shard_map/dot_general | solution.py:75
  10.2 3.1 %collective-permute-start = (bf16[1,384,256]{2,1,0:T(8,128)(2,1)S(1)}, bf16[1,384,256]{2,1,0:T(8,128)(2,1)S(1)}, u32[]{:S(2)}, u32[]{:S(2)}) collective-permute-start(bf16[1,384,256]{2,1,0:T(8,128)(2,1)S(1)} %bitcast.50), channel_id=1, source_target_pairs={{0,4},{4,0},{8,12},{12,8},{1,5},{5,1},{9,13},{13,9},{2,6},{6,2},{1... | collective-permute-start | bytes 589832 | tf_op jit(solution)/shard_map/ppermute | solution.py:23
  13.3 4.9 %collective-permute-done = bf16[1,384,256]{2,1,0:T(8,128)(2,1)S(1)} collective-permute-done((bf16[1,384,256]{2,1,0:T(8,128)(2,1)S(1)}, bf16[1,384,256]{2,1,0:T(8,128)(2,1)S(1)}, u32[]{:S(2)}, u32[]{:S(2)}) %collective-permute-start) | collective-permute-done | bytes 196640 | tf_op jit(solution)/shard_map/ppermute | solution.py:23
  18.2 0.1 fusion.40
  18.3 2.8 %collective-permute-start.1 = (bf16[2,384,256]{2,1,0:T(8,128)(2,1)S(1)}, bf16[2,384,256]{2,1,0:T(8,128)(2,1)S(1)}, u32[]{:S(2)}, u32[]{:S(2)}) collective-permute-start(bf16[2,384,256]{2,1,0:T(8,128)(2,1)S(1)} %get-tuple-element.10), channel_id=1, source_target_pairs={{0,8},{4,12},{8,0},{12,4},{1,9},{5,13},{9,1},{13,5},{2,10},{6,14},... | collective-permute-start | bytes 1179656 | tf_op jit(solution)/shard_map/ppermute | solution.py:23
  21.1 16.8 %collective-permute-done.1 = bf16[2,384,256]{2,1,0:T(8,128)(2,1)S(1)} collective-permute-done((bf16[2,384,256]{2,1,0:T(8,128)(2,1)S(1)}, bf16[2,384,256]{2,1,0:T(8,128)(2,1)S(1)}, u32[]{:S(2)}, u32[]{:S(2)}) %collective-permute-start.1) | collective-permute-done | bytes 393248 | tf_op jit(solution)/shard_map/ppermute | solution.py:23
  38.0 0.1 pad_maximum_fusion
  38.1 0.1 reverse_select_fusion
  38.2 0.7 fusion.23
  38.9 0.1 copy.19
  39.0 3.3 %fusion.59 = (f32[512,2]{0,1:T(2,128)S(1)}, f32[512,2,1024]{2,0,1:T(8,128)}) fusion(bf16[2,1024,256]{2,1,0:T(8,128)(2,1)S(1)} %copy-done, bf16[512,256]{1,0:T(8,128)(2,1)S(1)} %fusion.23), kind=kOutput, calls=%fused_computation.87 | convolution fusion | flops 540017664 | bytes 5509120 | tf_op jit(solution)/shard_map/sub | solution.py:91
  42.3 3.1 %multiply_reduce_fusion.3 = (f32[512,2]{0,1:T(2,128)S(1)}, f32[512,2,256]{0,2,1:T(8,128)S(1)}) fusion(bf16[2,1024,256]{2,1,0:T(8,128)(2,1)S(1)} %copy-done, f32[512,2,1024]{2,0,1:T(8,128)} %get-tuple-element.17, f32[512,2]{0,1:T(2,128)S(1)} %get-tuple-element.16), kind=kOutput, calls=%fused_computation.47 | convolution fusion | flops 539491328 | bytes 6299648 | tf_op jit(solution)/shard_map/qtp,tpc->qtc/dot_general | solution.py:93
  45.4 0.0 copy-start.2
  45.4 0.1 divide_convert_fusion.6
  45.6 0.8 copy-done.2
  46.4 0.8 multiply_reduce_fusion.2
  47.3 0.0 copy-start.1
  47.3 0.2 divide_convert_fusion.2
  47.5 0.1 fusion.57
  47.6 2.5 %collective-permute-start.2 = (bf16[512,1,512]{2,0,1:T(8,128)(2,1)S(1)}, bf16[512,1,512]{2,0,1:T(8,128)(2,1)S(1)}, u32[]{:S(2)}, u32[]{:S(2)}) collective-permute-start(bf16[512,1,512]{2,0,1:T(8,128)(2,1)S(1)} %get-tuple-element.7), channel_id=1, source_target_pairs={{0,4},{4,8},{8,12},{1,5},{5,9},{9,13},{2,6},{6,10},{10,14},{3,7},{... | collective-permute-start | bytes 1572872 | tf_op jit(solution)/shard_map/ppermute | solution.py:39
  50.1 1.5 %collective-permute-start.3 = (bf16[512,1,512]{2,0,1:T(8,128)(2,1)S(1)}, bf16[512,1,512]{2,0,1:T(8,128)(2,1)S(1)}, u32[]{:S(2)}, u32[]{:S(2)}) collective-permute-start(bf16[512,1,512]{2,0,1:T(8,128)(2,1)S(1)} %get-tuple-element.8), channel_id=1, source_target_pairs={{4,0},{8,4},{12,8},{5,1},{9,5},{13,9},{6,2},{10,6},{14,10},{7,3},{... | collective-permute-start | bytes 1572872 | tf_op jit(solution)/shard_map/ppermute | solution.py:41
  51.6 0.0 copy-done.1
  51.6 9.8 %collective-permute-done.2 = bf16[512,1,512]{2,0,1:T(8,128)(2,1)S(1)} collective-permute-done((bf16[512,1,512]{2,0,1:T(8,128)(2,1)S(1)}, bf16[512,1,512]{2,0,1:T(8,128)(2,1)S(1)}, u32[]{:S(2)}, u32[]{:S(2)}) %collective-permute-start.2) | collective-permute-done | bytes 524320 | tf_op jit(solution)/shard_map/ppermute | solution.py:39
  61.4 4.1 %collective-permute-done.3 = bf16[512,1,512]{2,0,1:T(8,128)(2,1)S(1)} collective-permute-done((bf16[512,1,512]{2,0,1:T(8,128)(2,1)S(1)}, bf16[512,1,512]{2,0,1:T(8,128)(2,1)S(1)}, u32[]{:S(2)}, u32[]{:S(2)}) %collective-permute-start.3) | collective-permute-done | bytes 524320 | tf_op jit(solution)/shard_map/ppermute | solution.py:41
  65.6 0.3 maximum_convert_fusion
  65.9 0.7 multiply_reduce_fusion.1
  66.6 0.2 divide_convert_fusion.1
  66.8 2.0 %copy.21 = bf16[512,2,512]{2,1,0:T(2,128)(2,1)} copy(bf16[512,2,512]{2,0,1:T(8,128)(2,1)S(1)} %divide_convert_fusion.1) | data formatting | bytes 2097152 | tf_op jit(solution)/shard_map/convert_element_type | solution.py:105
  68.9 2.3 %reshape.59 = bf16[1024,512]{1,0:T(8,128)(2,1)} reshape(bf16[512,2,512]{2,1,0:T(2,128)(2,1)} %copy.21) | data formatting | bytes 2097152 | tf_op jit(solution)/shard_map/reshape | solution.py:105
  71.1 5.3 %convolution_convert_fusion = bf16[1024,512]{1,0:T(8,128)(2,1)} fusion(bf16[1024,512]{1,0:T(8,128)(2,1)} %reshape.59, bf16[1,1024,512]{2,1,0:T(8,128)(2,1)} %param.13, bf16[1,512,1024]{2,1,0:T(8,128)(2,1)} %param.12), kind=kOutput, calls=%fused_computation.34 | convolution fusion | flops 2157445120 | bytes 4194304 | tf_op jit(solution)/shard_map/dot_general | solution.py:109
  76.4 2.3 %reshape.60 = bf16[512,2,512]{2,1,0:T(2,128)(2,1)} reshape(bf16[1024,512]{1,0:T(8,128)(2,1)} %convolution_convert_fusion) | data formatting | bytes 2097152 | tf_op jit(solution)/shard_map/reshape | solution.py:111
  78.6 2.4 %copy.22 = bf16[512,2,512]{2,0,1:T(8,128)(2,1)} copy(bf16[512,2,512]{2,1,0:T(2,128)(2,1)} %reshape.60) | data formatting | bytes 2097152 | tf_op jit(solution)/shard_map/reshape | solution.py:111
  81.0 0.0 all-reduce.2.cloned.1.call-update
  81.0 20.6 %all-reduce.2.cloned.1.call-done = bf16[512,2,512]{2,0,1:T(8,128)(2,1)} async-done(((bf16[512,2,512]{2,0,1:T(8,128)(2,1)}), bf16[512,2,512]{2,0,1:T(8,128)(2,1)}) %all-reduce.2.cloned.1.call-update) | async-done | bytes 1048592 | tf_op jit(solution)/shard_map/psum | solution.py:110
  101.6 1.6 %add_convert_fusion = bf16[512,2,512]{2,0,1:T(8,128)(2,1)S(1)} fusion(f32[512,2,512]{2,0,1:T(8,128)S(1)} %get-tuple-element.6, bf16[512,2,512]{2,0,1:T(8,128)(2,1)} %all-reduce.2.cloned.1.call-done), kind=kLoop, calls=%fused_computation.25 | loop fusion | flops 1572864 | bytes 4194304 | tf_op jit(solution)/shard_map/convert_element_type | solution.py:112
  103.2 2.0 %copy.23 = bf16[512,2,512]{2,1,0:T(2,128)(2,1)} copy(bf16[512,2,512]{2,0,1:T(8,128)(2,1)S(1)} %add_convert_fusion) | data formatting | bytes 2097152 | tf_op jit(solution)/shard_map/convert_element_type | solution.py:112
  (7 shorter events, 0.1 us)
Async XLA Ops:
  6.5 2.4 %copy-start = (bf16[2,1024,256]{2,1,0:T(8,128)(2,1)S(1)}, bf16[2,1024,256]{2,1,0:T(8,128)(2,1)}, u32[]{:S(2)}) copy-start(bf16[2,1024,256]{2,1,0:T(8,128)(2,1)} %param.7) | copy-start | bytes 3145732
  6.5 95.0 %all-reduce.2.cloned.1.call-start = ((), (), s32[]{:S(2)}) async-start(), calls=%async_computation | async-start | bytes 2097152 | tf_op jit(solution)/shard_map/psum | solution.py:110
  10.2 8.0 %collective-permute-start = (bf16[1,384,256]{2,1,0:T(8,128)(2,1)S(1)}, bf16[1,384,256]{2,1,0:T(8,128)(2,1)S(1)}, u32[]{:S(2)}, u32[]{:S(2)}) collective-permute-start(bf16[1,384,256]{2,1,0:T(8,128)(2,1)S(1)} %bitcast.50), channel_id=1, source_target_pairs={{0,4},{4,0},{8,12},{12,8},{1,5},{5,1},{9,13},{13,9},{2,6},{6,2},{1... | collective-permute-start | bytes 589832 | tf_op jit(solution)/shard_map/ppermute | solution.py:23
  18.3 19.7 %collective-permute-start.1 = (bf16[2,384,256]{2,1,0:T(8,128)(2,1)S(1)}, bf16[2,384,256]{2,1,0:T(8,128)(2,1)S(1)}, u32[]{:S(2)}, u32[]{:S(2)}) collective-permute-start(bf16[2,384,256]{2,1,0:T(8,128)(2,1)S(1)} %get-tuple-element.10), channel_id=1, source_target_pairs={{0,8},{4,12},{8,0},{12,4},{1,9},{5,13},{9,1},{13,5},{2,10},{6,14},... | collective-permute-start | bytes 1179656 | tf_op jit(solution)/shard_map/ppermute | solution.py:23
  45.4 1.0 copy-start.2
  47.3 4.3 %copy-start.1 = (f32[1,3,512]{2,0,1:T(1,128)S(1)}, f32[1,3,512]{2,0,1:T(1,128)}, u32[]{:S(2)}) copy-start(f32[1,3,512]{2,0,1:T(1,128)} %param.11) | copy-start | bytes 18436
  47.6 13.8 %collective-permute-start.2 = (bf16[512,1,512]{2,0,1:T(8,128)(2,1)S(1)}, bf16[512,1,512]{2,0,1:T(8,128)(2,1)S(1)}, u32[]{:S(2)}, u32[]{:S(2)}) collective-permute-start(bf16[512,1,512]{2,0,1:T(8,128)(2,1)S(1)} %get-tuple-element.7), channel_id=1, source_target_pairs={{0,4},{4,8},{8,12},{1,5},{5,9},{9,13},{2,6},{6,10},{10,14},{3,7},{... | collective-permute-start | bytes 1572872 | tf_op jit(solution)/shard_map/ppermute | solution.py:39
  50.1 15.5 %collective-permute-start.3 = (bf16[512,1,512]{2,0,1:T(8,128)(2,1)S(1)}, bf16[512,1,512]{2,0,1:T(8,128)(2,1)S(1)}, u32[]{:S(2)}, u32[]{:S(2)}) collective-permute-start(bf16[512,1,512]{2,0,1:T(8,128)(2,1)S(1)} %get-tuple-element.8), channel_id=1, source_target_pairs={{4,0},{8,4},{12,8},{5,1},{9,5},{13,9},{6,2},{10,6},{14,10},{7,3},{... | collective-permute-start | bytes 1572872 | tf_op jit(solution)/shard_map/ppermute | solution.py:41
Sparse Core Ops, SparseCore 0:
  81.1 20.4 all-reduce.1
